TPU v7x, 32 devices: a whole 2x2x4 slice. The times are simulated.
32 devices in a mesh: leaf: 8 (over z, x), vec: 4 (over y, core).
Axes of the slice: x: 2, y: 2, z: 4, core: 2. Of those that a mesh axis runs over, the one named last changes fastest.
Arguments:
- panels: float32 [32, 65536], P('vec', 'leaf'), may hold values from -6 to 6
- near_tiles: float32 [512, 4, 128, 128], P('leaf', None, 'vec'), may hold values from -0.25 to 0.25
- near_cols: int32 [512, 4], P('leaf'), may hold values from 0 to 511, as said below
- leaf_order: int32 [512, 128], P('leaf'), may hold values from 0 to 127, each once within a row
- leaf_basis: float32 [512, 64, 128], P('leaf'), may hold values from -0.5 to 0.5
- local_mats: float32 [8, 63, 64, 128], P('leaf'), may hold values from -0.75 to 0.75
- local_flags: int32 [8, 63], P('leaf'), may hold values 0 or 1
- cross_coupling: float32 [6, 64, 64], replicated, may hold values from -0.75 to 0.75
- cross_transfer: float32 [4, 64, 64], replicated, may hold values from -0.75 to 0.75
- cross_flags: int32 [6], replicated, may hold values 0 or 1
Outputs:
- product: float32 [32, 65536], P('vec', 'leaf')
Inputs may be any that keep to these rules, and one draw needn't show every extreme that they name: `near_cols`: every entry of row i names a leaf within 8 leaves of leaf i. `leaf_order`: each row is a permutation of 0 to 127.
All inputs are finite; a program needn't handle non-finite values. No bound on the sum of `local_flags` on one device may be relied on, other than what follows from the above.
Results may differ from a plain program's by a relative error of at most 0.00022.
Values sent between devices are 32-bit elements; how exact they have to be, the bound alone decides.
A program may use at most 64 MiB of HBM per device.

v0:
```python
import math
import jax
import jax.numpy as jnp
from jax import lax
from jax.sharding import PartitionSpec as P

W = 8
precise = lax.Precision.HIGHEST
root_half = 1.0 / math.sqrt(2.0)


def extended_2(cells, sides, width):
    for axis, dim in sides:
        count = lax.axis_size(axis)
        ends = count - 1
        head = lax.slice_in_dim(cells, 0, width, axis=dim)
        tail = lax.slice_in_dim(cells, cells.shape[dim] - width, cells.shape[dim], axis=dim)
        cells = jnp.concatenate(
            [
                lax.ppermute(tail, axis, [(i, (i + 1) % count) for i in range(ends)]),
                cells,
                lax.ppermute(head, axis, [((i + 1) % count, i) for i in range(ends)]),
            ],
            axis=dim,
        )
    return cells


def partner(block, axis, bit):
    count = lax.axis_size(axis)
    route = []
    for low in range(count):
        high = low | 1 << bit
        if high != low and high < count:
            route += [(low, high), (high, low)]
    return lax.ppermute(block, axis, route)


def near_product(tile_rows, sources):
    return jnp.einsum("lnqp,slnp->slq", tile_rows, sources, precision=precise)


def local(
    panels,
    near_tiles,
    near_cols,
    leaf_order,
    leaf_basis,
    local_mats,
    local_flags,
    cross_coupling,
    cross_transfer,
    cross_flags,
):
    rhs_dev = panels.shape[0]
    leaves = leaf_basis.shape[0]
    skel_rank = leaf_basis.shape[1]
    leaf_size = leaf_basis.shape[2]
    halo_cells = W * leaf_size
    leaf_count = lax.axis_size("leaf")
    leaf_index = lax.axis_index("leaf")
    cross_depth = leaf_count.bit_length() - 1
    places = jnp.arange(leaf_size, dtype=jnp.int32)
    order_hot = (leaf_order[:, :, None] == places[None, None, :]).astype(jnp.float32)
    ordered = jnp.einsum(
        "lpm,slm->slp", order_hot, panels.reshape(rhs_dev, leaves, leaf_size), precision=precise
    )
    ordered_flat = ordered.reshape(rhs_dev, leaves * leaf_size)
    local_cols = near_cols - leaf_index * leaves + W
    rim_leaves = jnp.arange(leaves + 2 * W, dtype=jnp.int32)
    select_hot = (local_cols[:, :, None] == rim_leaves[None, None, :]).astype(jnp.float32)
    gathered = lax.all_gather(ordered_flat, "vec", axis=0, tiled=True)
    extended = extended_2(gathered, (("leaf", 1),), halo_cells)
    blocked = extended.reshape(extended.shape[0], leaves + 2 * W, leaf_size)
    partial_rows = near_product(
        near_tiles, jnp.einsum("lne,sep->slnp", select_hot, blocked, precision=precise)
    )
    near_field = lax.all_to_all(partial_rows, "vec", split_axis=0, concat_axis=2, tiled=True)
    local_blocks = local_mats[0]
    local_admit = local_flags[0].astype(jnp.float32)
    leaf_skel = jnp.einsum("lkp,slp->lsk", leaf_basis, ordered, precision=precise)
    skeleton = leaf_skel.reshape(leaves // 2, 2, rhs_dev, skel_rank).sum(axis=1) * root_half
    local_depth = leaves.bit_length() - 1
    coupled = []
    for tree_level in range(1, local_depth):
        node_count = leaves >> tree_level
        first_node = leaves - (leaves >> tree_level - 1)
        blocks = local_blocks[first_node : first_node + node_count]
        sibling = skeleton.reshape(node_count // 2, 2, rhs_dev, skel_rank)[:, ::-1].reshape(
            skeleton.shape
        )
        term = jnp.einsum("jkm,jsm->jsk", blocks[:, :, :skel_rank], sibling, precision=precise)
        coupled.append(local_admit[first_node : first_node + node_count, None, None] * term)
        lifted = jnp.einsum("jsk,jkm->jsm", skeleton, blocks[:, :, skel_rank:], precision=precise)
        skeleton = lifted.reshape(node_count // 2, 2, rhs_dev, skel_rank).sum(axis=1) * root_half
    device_block = local_blocks[leaves - 2]
    device_skel = skeleton[0]
    device_lift = jnp.dot(device_skel, device_block[:, skel_rank:], precision=precise)

    def cross_index(level_bit):
        return leaf_count - (leaf_count >> level_bit - 1) + (leaf_index >> level_bit)

    def transfer_at(level_bit):
        if level_bit == 0:
            return device_block[:, skel_rank:]
        return lax.dynamic_index_in_dim(cross_transfer, cross_index(level_bit), 0, keepdims=False)

    cross_terms = []
    current, carried = (device_skel, device_lift)
    for level_bit in range(cross_depth):
        sibling_skel, sibling_up = partner((current, carried), "leaf", level_bit)
        if level_bit == 0:
            coupling = device_block[:, :skel_rank]
            admitted = local_admit[leaves - 2]
        else:
            node_index = cross_index(level_bit)
            coupling = lax.dynamic_index_in_dim(cross_coupling, node_index, 0, keepdims=False)
            admitted = lax.dynamic_index_in_dim(cross_flags, node_index, 0, keepdims=False).astype(
                jnp.float32
            )
        cross_terms.append(admitted * jnp.dot(sibling_skel, coupling.T, precision=precise))
        if level_bit < cross_depth - 1:
            current = (carried + sibling_up) * root_half
            if level_bit + 1 <= cross_depth - 2:
                carried = jnp.dot(current, transfer_at(level_bit + 1), precision=precise)
    downward = cross_terms[cross_depth - 1]
    for level_bit in range(cross_depth - 2, -1, -1):
        downward = cross_terms[level_bit] + jnp.dot(
            downward, transfer_at(level_bit).T, precision=precise
        )
    downward = downward[None]
    for tree_level in range(local_depth - 1, 0, -1):
        node_count = leaves >> tree_level
        first_node = leaves - (leaves >> tree_level - 1)
        transfer = local_blocks[first_node : first_node + node_count, :, skel_rank:]
        spread = jnp.repeat(downward, 2, axis=0)
        downward = coupled[tree_level - 1] + jnp.einsum(
            "jkm,jsm->jsk", transfer, spread, precision=precise
        )
    far_field = jnp.einsum(
        "lkp,lsk->slp", leaf_basis, jnp.repeat(downward, 2, axis=0), precision=precise
    )
    combined = near_field + far_field
    restored = jnp.einsum("lpm,slp->slm", order_hot, combined, precision=precise)
    return restored.reshape(rhs_dev, leaves * leaf_size)


def solution(mesh):
    return jax.shard_map(
        local,
        mesh=mesh,
        in_specs=(
            P("vec", "leaf"),
            P("leaf", None, "vec", None),
            P("leaf", None),
            P("leaf", None),
            P("leaf", None, None),
            P("leaf", None, None, None),
            P("leaf", None),
            P(),
            P(),
            P(),
        ),
        out_specs=P("vec", "leaf"),
        check_vma=False,
    )
```

profile of v0, /device:TPU:0, one launch (start us, length us, event | category | flops | bytes accessed | tf_op | source)
XLA Modules:
  0.0 107.7 jit_solution(1029454340300619483)
XLA Ops:
  6.5 1.4 %slice_bitcast_fusion = f32[32,64,128]{2,1,0:T(8,128)S(1)} fusion(f32[1,63,64,128]{3,2,1,0:T(8,128)} %param.15), kind=kLoop, calls=%fused_computation.34 | loop fusion | bytes 2097152 | tf_op jit(solution)/shard_map/slice | solution.py:88
  9.1 1.2 %slice_bitcast_fusion.2 = f32[8,64,128]{2,1,0:T(8,128)S(1)} fusion(f32[1,63,64,128]{3,2,1,0:T(8,128)} %param.15), kind=kLoop, calls=%fused_computation.48 | loop fusion | bytes 524288 | tf_op jit(solution)/shard_map/slice | solution.py:88
  12.1 4.7 %fusion.2 = f32[64,128,8]{1,2,0:T(8,128)S(1)} fusion(s32[64,128]{1,0:T(8,128)S(1)} %copy-done.18, f32[8,8192]{1,0:T(8,128)S(1)} %copy-done.17), kind=kOutput, calls=%fused_computation.4 | convolution fusion | flops 101711872 | bytes 557056 | tf_op jit(solution)/shard_map/lpm,slm->slp/dot_general | solution.py:65
  16.9 3.4 %bitcast_reduce_fusion = f32[32,8,64]{2,1,0:T(8,128)S(1)} fusion(f32[64,64,128]{2,1,0:T(8,128)S(1)} %copy-done, f32[64,128,8]{1,2,0:T(8,128)S(1)} %fusion.2), kind=kOutput, calls=%fused_computation.44 | convolution fusion | flops 50348032 | bytes 2424832 | tf_op jit(solution)/shard_map/lkp,slp->lsk/dot_general | solution.py:81
  20.2 1.2 %bitcast_reduce_fusion.1 = f32[16,8,64]{2,1,0:T(8,128)S(1)} fusion(f32[32,64,128]{2,1,0:T(8,128)S(1)} %slice_bitcast_fusion, f32[32,8,64]{2,1,0:T(8,128)S(1)} %bitcast_reduce_fusion), kind=kOutput, calls=%fused_computation.53 | convolution fusion | flops 12607488 | bytes 1146880 | tf_op jit(solution)/shard_map/jsk,jkm->jsm/dot_general | solution.py:94
  23.7 3.0 %collective-permute-start.2 = (f32[8,64]{1,0:T(8,128)}, f32[8,64]{1,0:T(8,128)}, u32[]{:S(2)}, u32[]{:S(2)}) collective-permute-start(f32[8,64]{1,0:T(8,128)} %fusion.12), channel_id=1, source_target_pairs={{0,4},{4,0},{8,12},{12,8},{16,20},{20,16},{24,28},{28,24},{1,5},{5... | collective-permute-start | bytes 6152 | tf_op jit(solution)/shard_map/ppermute | solution.py:36
  28.0 1.5 %fusion.68 = f32[8,64]{1,0:T(8,128)} fusion(f32[8,64]{1,0:T(8,128)} %fusion.12, f32[64,128]{1,0:T(8,128)S(1)} %slice_bitcast_fusion.5), kind=kOutput, calls=%fused_computation.84 | convolution fusion | flops 393216 | bytes 36864 | tf_op jit(solution)/shard_map/dot_general | solution.py:98
  32.1 1.9 %convolution_multiply_fusion.3 = f32[4,8,64]{2,1,0:T(8,128)} fusion(f32[4,8,64]{2,1,0:T(8,128)S(1)} %bitcast.147, f32[4,64,128]{2,1,0:T(8,128)} %copy-done.4, f32[4]{0:T(128)S(1)} %slice_bitcast_fusion.7), kind=kOutput, calls=%fused_computation.20 | convolution fusion | flops 1574912 | bytes 147472 | tf_op jit(solution)/shard_map/jkm,jsm->jsk/dot_general | solution.py:92
  34.5 2.0 %convolution_multiply_fusion.1 = f32[16,8,64]{2,1,0:T(8,128)S(1)} fusion(f32[16,8,64]{2,1,0:T(8,128)S(1)} %bitcast.142, f32[16,64,128]{2,1,0:T(8,128)} %copy-done.1, f32[16]{0:T(128)S(1)} %slice_bitcast_fusion.9), kind=kOutput, calls=%fused_computation.16 | convolution fusion | flops 6299648 | bytes 589888 | tf_op jit(solution)/shard_map/jkm,jsm->jsk/dot_general | solution.py:92
  36.5 1.8 %convolution_multiply_fusion = f32[32,8,64]{2,1,0:T(8,128)S(1)} fusion(f32[32,8,64]{2,1,0:T(8,128)S(1)} %bitcast.139, f32[32,64,128]{2,1,0:T(8,128)S(1)} %slice_bitcast_fusion, f32[32]{0:T(128)S(1)} %slice_bitcast_fusion.10), kind=kOutput, calls=%fused_computation.14 | convolution fusion | flops 12599296 | bytes 1179776 | tf_op jit(solution)/shard_map/jkm,jsm->jsk/dot_general | solution.py:92
  39.9 2.1 %collective-permute-start.5 = (f32[8,64]{1,0:T(8,128)S(1)}, f32[8,64]{1,0:T(8,128)S(1)}, u32[]{:S(2)}, u32[]{:S(2)}) collective-permute-start(f32[8,64]{1,0:T(8,128)S(1)} %fusion.55), channel_id=1, source_target_pairs={{0,8},{8,0},{4,12},{12,4},{16,24},{24,16},{20,28},{28,20},{1,9},{9... | collective-permute-start | bytes 6152 | tf_op jit(solution)/shard_map/ppermute | solution.py:36
  42.2 1.4 %collective-permute-done.5 = f32[8,64]{1,0:T(8,128)S(1)} collective-permute-done((f32[8,64]{1,0:T(8,128)S(1)}, f32[8,64]{1,0:T(8,128)S(1)}, u32[]{:S(2)}, u32[]{:S(2)}) %collective-permute-start.5) | collective-permute-done | bytes 2080 | tf_op jit(solution)/shard_map/ppermute | solution.py:36
  43.6 3.0 %collective-permute-start.6 = (f32[8,64]{1,0:T(8,128)S(1)}, f32[8,64]{1,0:T(8,128)S(1)}, u32[]{:S(2)}, u32[]{:S(2)}) collective-permute-start(f32[8,64]{1,0:T(8,128)S(1)} %add_multiply_fusion), channel_id=1, source_target_pairs={{0,16},{16,0},{4,20},{20,4},{8,24},{24,8},{12,28},{28,12},{1,17},{... | collective-permute-start | bytes 6152 | tf_op jit(solution)/shard_map/ppermute | solution.py:36
  46.6 1.2 %slice.157 = f32[1,1]{1,0:T(1,128)} slice(f32[1,63]{1,0:T(1,128)} %copy-done.20), slice={[0:1], [62:63]} | slice | bytes 8 | tf_op jit(solution)/shard_map/slice | solution.py:114
  49.8 1.6 %collective-permute-start.4 = (f32[8,64]{1,0:T(8,128)S(1)}, f32[8,64]{1,0:T(8,128)S(1)}, u32[]{:S(2)}, u32[]{:S(2)}) collective-permute-start(f32[8,64]{1,0:T(8,128)S(1)} %add_multiply_fusion.1), channel_id=1, source_target_pairs={{0,8},{8,0},{4,12},{12,4},{16,24},{24,16},{20,28},{28,20},{1,9},{9... | collective-permute-start | bytes 6152 | tf_op jit(solution)/shard_map/ppermute | solution.py:36
  54.6 1.4 %fusion.11 = f32[8,64]{1,0:T(8,128)S(1)} fusion(f32[8,64]{1,0:T(8,128)S(1)} %fusion.66, f32[8,64]{1,0:T(8,128)} %collective-permute-done.2, f32[64,128]{1,0:T(8,128)S(1)} %copy-done.10, f32[]{:T(128)} %bitcast.35), kind=kOutput, calls=%fused_computation.27 | convolution fusion | flops 394240 | bytes 38916 | tf_op jit(solution)/shard_map/dot_general | solution.py:121
  57.1 1.3 %convolution_add_fusion.3 = f32[4,8,64]{2,1,0:T(8,128)S(1)} fusion(f32[4,8,64]{2,1,0:T(8,128)S(1)} %copy-done.14, f32[4,8,64]{2,1,0:T(8,128)S(1)} %bitcast.148, f32[63,64,128]{2,1,0:T(8,128)} %bitcast.127), kind=kOutput, calls=%fused_computation.19 | convolution fusion | flops 1574912 | bytes 155648 | tf_op jit(solution)/shard_map/jkm,jsm->jsk/dot_general | solution.py:137
  58.5 1.5 %convolution_add_fusion.2 = f32[8,8,64]{2,1,0:T(8,128)S(1)} fusion(f32[8,8,64]{2,1,0:T(8,128)S(1)} %convolution_multiply_fusion.2, f32[8,8,64]{2,1,0:T(8,128)S(1)} %bitcast.146, f32[63,64,128]{2,1,0:T(8,128)} %bitcast.128), kind=kOutput, calls=%fused_computation.17 | convolution fusion | flops 3149824 | bytes 311296 | tf_op jit(solution)/shard_map/jkm,jsm->jsk/dot_general | solution.py:137
  61.1 3.4 %collective-permute-start = (f32[32,1024]{1,0:T(8,128)S(1)}, f32[32,1024]{1,0:T(8,128)S(1)}, u32[]{:S(2)}, u32[]{:S(2)}) collective-permute-start(f32[32,1024]{1,0:T(8,128)S(1)} %get-tuple-element.5), channel_id=1, source_target_pairs={{0,4},{4,8},{8,12},{12,16},{16,20},{20,24},{24,28},{1,5},{5,9},{9,... | collective-permute-start | bytes 393224 | tf_op jit(solution)/shard_map/ppermute | solution.py:20
  64.5 1.5 %collective-permute-start.1 = (f32[32,1024]{1,0:T(8,128)S(1)}, f32[32,1024]{1,0:T(8,128)S(1)}, u32[]{:S(2)}, u32[]{:S(2)}) collective-permute-start(f32[32,1024]{1,0:T(8,128)S(1)} %get-tuple-element.6), channel_id=1, source_target_pairs={{4,0},{8,4},{12,8},{16,12},{20,16},{24,20},{28,24},{5,1},{9,5},{13... | collective-permute-start | bytes 393224 | tf_op jit(solution)/shard_map/ppermute | solution.py:22
  66.0 2.0 %convolution_add_fusion.1 = f32[16,8,64]{2,1,0:T(8,128)S(1)} fusion(f32[16,8,64]{2,1,0:T(8,128)S(1)} %convolution_multiply_fusion.1, f32[16,8,64]{2,1,0:T(8,128)S(1)} %bitcast.143, f32[63,64,128]{2,1,0:T(8,128)} %bitcast.129), kind=kOutput, calls=%fused_computation.15 | convolution fusion | flops 6299648 | bytes 622592 | tf_op jit(solution)/shard_map/jkm,jsm->jsk/dot_general | solution.py:137
  68.4 3.0 %collective-permute-done.1 = f32[32,1024]{1,0:T(8,128)S(1)} collective-permute-done((f32[32,1024]{1,0:T(8,128)S(1)}, f32[32,1024]{1,0:T(8,128)S(1)}, u32[]{:S(2)}, u32[]{:S(2)}) %collective-permute-start.1) | collective-permute-done | bytes 131104 | tf_op jit(solution)/shard_map/ppermute | solution.py:22
  71.7 1.9 %convolution_bitcast_fusion.1 = f32[32,64,4,128]{3,1,2,0:T(8,128)S(1)} fusion(f32[32,80,128,1]{2,1,0,3:T(8,128)S(1)} %bitcast.131, s32[64,4]{0,1:T(4,128)S(1)} %subtract_add_fusion), kind=kOutput, calls=%fused_computation.5 | convolution fusion | flops 1006653440 | bytes 5506048 | tf_op jit(solution)/shard_map/lne,sep->slnp/dot_general | solution.py:76
  73.9 6.2 %fusion.5 = f32[32,64,32]{2,0,1:T(8,128)S(1)} fusion(f32[64,4,32,128]{3,2,1,0:T(8,128)S(1)} %copy-done.2, f32[32,64,4,128]{3,1,2,0:T(8,128)S(1)} %convolution_bitcast_fusion.1), kind=kOutput, calls=%fused_computation.8 | convolution fusion | flops 402653184 | bytes 8650752 | tf_op jit(solution)/shard_map/lnqp,slnp->slq/dot_general | solution.py:40
  80.1 1.4 %copy.17 = f32[32,64,32]{1,2,0:T(8,128)} copy(f32[32,64,32]{2,0,1:T(8,128)S(1)} %fusion.5) | data formatting | bytes 524288 | tf_op jit(solution)/shard_map/lnqp,slnp->slq/transpose | solution.py:40
  81.5 2.1 %reshape.130 = f32[4,1,16384]{2,1,0:T(1,128)} reshape(f32[32,32,64]{2,1,0:T(8,128)} %bitcast.132) | data formatting | bytes 524288
  83.6 3.6 %all-to-all-start = ((f32[4,1,16384]{2,1,0:T(1,128)}), f32[4,1,16384]{2,1,0:T(1,128)S(1)}, u32[]{:S(2)}, u32[]{:S(2)}) async-start(f32[4,1,16384]{2,1,0:T(1,128)} %reshape.130), calls=%async_computation | async-start | bytes 524288 | tf_op jit(solution)/shard_map/all_to_all | solution.py:78
  87.2 3.0 %convolution_add_fusion = f32[32,8,64]{2,1,0:T(8,128)S(1)} fusion(f32[32,8,64]{2,1,0:T(8,128)S(1)} %convolution_multiply_fusion, f32[32,8,64]{2,1,0:T(8,128)S(1)} %bitcast.140, f32[63,64,128]{2,1,0:T(8,128)} %bitcast.130), kind=kOutput, calls=%fused_computation.13 | convolution fusion | flops 12599296 | bytes 1245184 | tf_op jit(solution)/shard_map/jkm,jsm->jsk/dot_general | solution.py:137
  90.3 2.7 %all-to-all-done = f32[4,1,16384]{2,1,0:T(1,128)S(1)} async-done(((f32[4,1,16384]{2,1,0:T(1,128)}), f32[4,1,16384]{2,1,0:T(1,128)S(1)}, u32[]{:S(2)}, u32[]{:S(2)}) %all-to-all-start) | async-done | bytes 262176 | tf_op jit(solution)/shard_map/all_to_all | solution.py:78
  93.5 1.4 %reduce.2 = f32[4,16384]{1,0:T(4,128)S(1)} reduce(f32[4,1,16384]{2,1,0:T(1,128)S(1)} %all-to-all-done, f32[]{:T(128)} %broadcast.17), dimensions={1}, to_apply=%all_to_all.13.reduce_sub_computation | reduce | bytes 524292 | tf_op jit(solution)/shard_map/all_to_all | solution.py:78
  95.4 1.9 %fusion.9 = f32[8,64,128]{2,0,1:T(8,128)S(1)} fusion(f32[8,64,128]{2,0,1:T(8,128)S(1)} %copy.19, f32[64,8,64]{2,1,0:T(8,128)S(1)} %bitcast.137, f32[64,64,128]{2,1,0:T(8,128)S(1)} %copy-done), kind=kOutput, calls=%fused_computation.12 | convolution fusion | flops 50397184 | bytes 2752512 | tf_op jit(solution)/shard_map/lkp,lsk->slp/dot_general | solution.py:140
  97.3 3.6 %convolution_bitcast_fusion = f32[8,8192]{1,0:T(8,128)} fusion(f32[8,64,128]{2,0,1:T(8,128)S(1)} %fusion.9, s32[64,128]{1,0:T(8,128)S(1)} %copy-done.19), kind=kOutput, calls=%fused_computation | convolution fusion | flops 101711872 | bytes 557056 | tf_op jit(solution)/shard_map/lpm,slp->slm/dot_general | solution.py:144
  (94 shorter events, 19.5 us)
Async XLA Ops:
  6.5 10.3 %copy-start = (f32[64,64,128]{2,1,0:T(8,128)S(1)}, f32[64,64,128]{2,1,0:T(8,128)}, u32[]{:S(2)}) copy-start(f32[64,64,128]{2,1,0:T(8,128)} %param.14) | copy-start | bytes 6291460
  6.5 5.5 %copy-start.18 = (s32[64,128]{1,0:T(8,128)S(1)}, s32[64,128]{1,0:T(8,128)}, u32[]{:S(2)}) copy-start(s32[64,128]{1,0:T(8,128)} %param.13) | copy-start | bytes 98308
  6.5 53.5 %all-gather.2.cloned.1.call-start = ((), (), s32[]{:S(2)}) async-start(), calls=%async_computation.1 | async-start | bytes 1310720 | tf_op jit(solution)/shard_map/all_gather | solution.py:72
  6.5 5.5 %copy-start.17 = (f32[8,8192]{1,0:T(8,128)S(1)}, f32[8,8192]{1,0:T(8,128)}, u32[]{:S(2)}) copy-start(f32[8,8192]{1,0:T(8,128)} %param.10) | copy-start | bytes 786436
  9.1 12.3 %copy-start.1 = (f32[16,64,128]{2,1,0:T(8,128)}, f32[16,64,128]{2,1,0:T(8,128)S(1)}, u32[]{:S(2)}) copy-start(f32[16,64,128]{2,1,0:T(8,128)S(1)} %slice_bitcast_fusion.1) | copy-start | bytes 1572868
  11.2 11.3 %copy-start.4 = (f32[4,64,128]{2,1,0:T(8,128)}, f32[4,64,128]{2,1,0:T(8,128)S(1)}, u32[]{:S(2)}) copy-start(f32[4,64,128]{2,1,0:T(8,128)S(1)} %slice_bitcast_fusion.3) | copy-start | bytes 393220
  12.1 10.7 %copy-start.7 = (f32[2,64,128]{2,1,0:T(8,128)}, f32[2,64,128]{2,1,0:T(8,128)S(1)}, u32[]{:S(2)}) copy-start(f32[2,64,128]{2,1,0:T(8,128)S(1)} %slice_bitcast_fusion.4) | copy-start | bytes 196612
  16.9 5.2 %copy-start.5 = (f32[64,128,8]{1,2,0:T(8,128)}, f32[64,128,8]{1,2,0:T(8,128)S(1)}, u32[]{:S(2)}) copy-start(f32[64,128,8]{1,2,0:T(8,128)S(1)} %fusion.2) | copy-start | bytes 786436
  21.4 1.4 %copy-start.6 = (f32[16,8,64]{2,1,0:T(8,128)}, f32[16,8,64]{2,1,0:T(8,128)S(1)}, u32[]{:S(2)}) copy-start(f32[16,8,64]{2,1,0:T(8,128)S(1)} %bitcast_reduce_fusion.1) | copy-start | bytes 98308
  22.1 1.6 %copy-start.11 = (f32[8,8,64]{2,1,0:T(8,128)}, f32[8,8,64]{2,1,0:T(8,128)S(1)}, u32[]{:S(2)}) copy-start(f32[8,8,64]{2,1,0:T(8,128)S(1)} %bitcast_reduce_fusion.2) | copy-start | bytes 49156
  22.8 6.7 %copy-start.12 = (f32[2,8,64]{2,1,0:T(8,128)}, f32[2,8,64]{2,1,0:T(8,128)S(1)}, u32[]{:S(2)}) copy-start(f32[2,8,64]{2,1,0:T(8,128)S(1)} %bitcast_reduce_fusion.4) | copy-start | bytes 12292
  23.7 30.9 %collective-permute-start.2 = (f32[8,64]{1,0:T(8,128)}, f32[8,64]{1,0:T(8,128)}, u32[]{:S(2)}, u32[]{:S(2)}) collective-permute-start(f32[8,64]{1,0:T(8,128)} %fusion.12), channel_id=1, source_target_pairs={{0,4},{4,0},{8,12},{12,8},{16,20},{20,16},{24,28},{28,24},{1,5},{5... | collective-permute-start | bytes 6152 | tf_op jit(solution)/shard_map/ppermute | solution.py:36
  27.4 0.6 copy-start.9
  29.5 8.8 %collective-permute-start.3 = (f32[8,64]{1,0:T(8,128)}, f32[8,64]{1,0:T(8,128)}, u32[]{:S(2)}, u32[]{:S(2)}) collective-permute-start(f32[8,64]{1,0:T(8,128)} %fusion.68), channel_id=1, source_target_pairs={{0,4},{4,0},{8,12},{12,8},{16,20},{20,16},{24,28},{28,24},{1,5},{5... | collective-permute-start | bytes 6152 | tf_op jit(solution)/shard_map/ppermute | solution.py:36
  30.2 8.1 %copy-start.20 = (f32[1,63]{1,0:T(1,128)}, f32[1,63]{1,0:T(1,128)S(1)}, u32[]{:S(2)}) copy-start(f32[1,63]{1,0:T(1,128)S(1)} %convert_element_type.18) | copy-start | bytes 760
  30.4 7.9 %copy-start.13 = (f32[2,8,64]{2,1,0:T(8,128)S(1)}, f32[2,8,64]{2,1,0:T(8,128)}, u32[]{:S(2)}) copy-start(f32[2,8,64]{2,1,0:T(8,128)} %copy-done.12) | copy-start | bytes 12292
  30.4 16.2 %copy-start.16 = (s32[64,4]{0,1:T(4,128)S(1)}, s32[64,4]{0,1:T(4,128)}, u32[]{:S(2)}) copy-start(s32[64,4]{0,1:T(4,128)} %param.12) | copy-start | bytes 3076
  30.4 17.5 %copy-start.15 = (s32[6]{0:T(128)S(1)}, s32[6]{0:T(128)}, u32[]{:S(2)}) copy-start(s32[6]{0:T(128)} %param.19) | copy-start | bytes 76
  32.1 9.9 %copy-start.8 = (f32[2,64,128]{2,1,0:T(8,128)S(1)}, f32[2,64,128]{2,1,0:T(8,128)}, u32[]{:S(2)}) copy-start(f32[2,64,128]{2,1,0:T(8,128)} %copy-done.7) | copy-start | bytes 196612
  32.1 22.2 %copy-start.10 = (f32[64,128]{1,0:T(8,128)S(1)}, f32[64,128]{1,0:T(8,128)}, u32[]{:S(2)}) copy-start(f32[64,128]{1,0:T(8,128)} %copy-done.9) | copy-start | bytes 98308
  34.5 22.7 %copy-start.14 = (f32[4,8,64]{2,1,0:T(8,128)S(1)}, f32[4,8,64]{2,1,0:T(8,128)}, u32[]{:S(2)}) copy-start(f32[4,8,64]{2,1,0:T(8,128)} %convolution_multiply_fusion.3) | copy-start | bytes 24580
  39.9 3.7 %collective-permute-start.5 = (f32[8,64]{1,0:T(8,128)S(1)}, f32[8,64]{1,0:T(8,128)S(1)}, u32[]{:S(2)}, u32[]{:S(2)}) collective-permute-start(f32[8,64]{1,0:T(8,128)S(1)} %fusion.55), channel_id=1, source_target_pairs={{0,8},{8,0},{4,12},{12,4},{16,24},{24,16},{20,28},{28,20},{1,9},{9... | collective-permute-start | bytes 6152 | tf_op jit(solution)/shard_map/ppermute | solution.py:36
  43.6 7.8 %collective-permute-start.6 = (f32[8,64]{1,0:T(8,128)S(1)}, f32[8,64]{1,0:T(8,128)S(1)}, u32[]{:S(2)}, u32[]{:S(2)}) collective-permute-start(f32[8,64]{1,0:T(8,128)S(1)} %add_multiply_fusion), channel_id=1, source_target_pairs={{0,16},{16,0},{4,20},{20,4},{8,24},{24,8},{12,28},{28,12},{1,17},{... | collective-permute-start | bytes 6152 | tf_op jit(solution)/shard_map/ppermute | solution.py:36
  49.8 3.7 %collective-permute-start.4 = (f32[8,64]{1,0:T(8,128)S(1)}, f32[8,64]{1,0:T(8,128)S(1)}, u32[]{:S(2)}, u32[]{:S(2)}) collective-permute-start(f32[8,64]{1,0:T(8,128)S(1)} %add_multiply_fusion.1), channel_id=1, source_target_pairs={{0,8},{8,0},{4,12},{12,4},{16,24},{24,16},{20,28},{28,20},{1,9},{9... | collective-permute-start | bytes 6152 | tf_op jit(solution)/shard_map/ppermute | solution.py:36
  60.0 11.4 %copy-start.3 = (f32[32,8192]{1,0:T(8,128)S(1)}, f32[32,8192]{1,0:T(8,128)}, u32[]{:S(2)}) copy-start(f32[32,8192]{1,0:T(8,128)} %all-gather.2.cloned.1.call-done) | copy-start | bytes 3145732
  61.1 7.3 %collective-permute-start = (f32[32,1024]{1,0:T(8,128)S(1)}, f32[32,1024]{1,0:T(8,128)S(1)}, u32[]{:S(2)}, u32[]{:S(2)}) collective-permute-start(f32[32,1024]{1,0:T(8,128)S(1)} %get-tuple-element.5), channel_id=1, source_target_pairs={{0,4},{4,8},{8,12},{12,16},{16,20},{20,24},{24,28},{1,5},{5,9},{9,... | collective-permute-start | bytes 393224 | tf_op jit(solution)/shard_map/ppermute | solution.py:20
  64.5 6.9 %collective-permute-start.1 = (f32[32,1024]{1,0:T(8,128)S(1)}, f32[32,1024]{1,0:T(8,128)S(1)}, u32[]{:S(2)}, u32[]{:S(2)}) collective-permute-start(f32[32,1024]{1,0:T(8,128)S(1)} %get-tuple-element.6), channel_id=1, source_target_pairs={{4,0},{8,4},{12,8},{16,12},{20,16},{24,20},{28,24},{5,1},{9,5},{13... | collective-permute-start | bytes 393224 | tf_op jit(solution)/shard_map/ppermute | solution.py:22
  71.7 2.2 %copy-start.2 = (f32[64,4,32,128]{3,2,1,0:T(8,128)S(1)}, f32[64,4,32,128]{3,2,1,0:T(8,128)}, u32[]{:S(2)}) copy-start(f32[64,4,32,128]{3,2,1,0:T(8,128)} %param.11) | copy-start | bytes 12582916
  83.6 9.4 %all-to-all-start = ((f32[4,1,16384]{2,1,0:T(1,128)}), f32[4,1,16384]{2,1,0:T(1,128)S(1)}, u32[]{:S(2)}, u32[]{:S(2)}) async-start(f32[4,1,16384]{2,1,0:T(1,128)} %reshape.130), calls=%async_computation | async-start | bytes 524288 | tf_op jit(solution)/shard_map/all_to_all | solution.py:78
  95.2 2.1 %copy-start.19 = (s32[64,128]{1,0:T(8,128)S(1)}, s32[64,128]{1,0:T(8,128)}, u32[]{:S(2)}) copy-start(s32[64,128]{1,0:T(8,128)} %param.13) | copy-start | bytes 98308
Sparse Core Ops, SparseCore 0:
  29.6 18.5 all-gather.1
where the time goes:
time: 109 us; the launch traced here: 108 us
  matrix products  47.1 us (43%)
  starting transfers between devices  18.3 us (17%)
  local copies, waits for them, and re-layouts  15.3 us (14%)
  between operations  15 us (14%)
  waiting for transfers between devices  7.65 us (7%)
  other arithmetic  4.46 us (4%)
    ppermute x5, starting transfers between devices, partner(): return lax.ppermute(block, axis, route)  9.76 us
    dot_general x5, matrix products, local(): jnp.einsum('jkm,jsm->jsk', transfer, spread, precision=precise)  9.07 us
    dot_general x5, matrix products, local(): jnp.einsum('jkm,jsm->jsk', blocks[:, :, :skel_rank], sibling, precision=p...  6.3 us
    dot_general x1, matrix products, near_product(): return jnp.einsum('lnqp,slnp->slq', tile_rows, sources, precision=precise)  6.21 us
    slice x5, local copies, waits for them, and re-layouts, local(): blocks = local_blocks[first_node:first_node + node_count]  5.5 us
    dot_general x1, matrix products, local(): jnp.einsum('lpm,slm->slp', order_hot, panels.reshape(rhs_dev, leaves, lea...  4.75 us
    all_to_all x1, starting transfers between devices, local(): lax.all_to_all(partial_rows, 'vec', split_axis=0, concat_axis=2, tiled=True)  3.63 us
    unnamed x45, local copies, waits for them, and re-layouts  3.58 us
  transfers between devices with their start and end apart: 9, of which 5 were waited for; matrix products, arithmetic and copies ran while one was open for 26% of the time, Pallas kernels for 0%

commit v1 on v0

--- a/solution.py
+++ b/solution.py
@@ -75,7 +75,12 @@
     partial_rows = near_product(
         near_tiles, jnp.einsum("lne,sep->slnp", select_hot, blocked, precision=precise)
     )
-    near_field = lax.all_to_all(partial_rows, "vec", split_axis=0, concat_axis=2, tiled=True)
+    near_field = jnp.concatenate(
+        jax.lax.all_to_all(
+            jnp.stack(jnp.split(partial_rows, jax.lax.axis_size("vec"), 0), 0), "vec", 0, 0
+        ),
+        2,
+    )
     local_blocks = local_mats[0]
     local_admit = local_flags[0].astype(jnp.float32)
     leaf_skel = jnp.einsum("lkp,slp->lsk", leaf_basis, ordered, precision=precise)

time: 109 us -> 109 us (level)
    transpose x1 -> x0, local copies, waits for them, and re-layouts: 1.39 us -> none  [near_product(): return jnp.einsum('lnqp,slnp->slq', tile_rows, sources, precision=precise)]
    another operation x1 -> x3, local copies, waits for them, and re-layouts: 0.01 us -> 1.23 us  [the longest x2 1.22 us: local(): jnp.stack(jnp.split(partial_rows, jax.lax.axis_size('vec'), 0), 0)]
where the time goes in v1:
time: 109 us; the launch traced here: 108 us
  matrix products  47.2 us (43%)
  starting transfers between devices  18.3 us (17%)
  local copies, waits for them, and re-layouts  15.1 us (14%)
  between operations  15 us (14%)
  waiting for transfers between devices  7.64 us (7%)
  other arithmetic  4.53 us (4%)
    ppermute x5, starting transfers between devices, partner(): return lax.ppermute(block, axis, route)  9.76 us
    dot_general x5, matrix products, local(): jnp.einsum('jkm,jsm->jsk', transfer, spread, precision=precise)  9.07 us
    dot_general x5, matrix products, local(): jnp.einsum('jkm,jsm->jsk', blocks[:, :, :skel_rank], sibling, precision=p...  6.31 us
    dot_general x1, matrix products, near_product(): return jnp.einsum('lnqp,slnp->slq', tile_rows, sources, precision=precise)  6.25 us
    slice x5, local copies, waits for them, and re-layouts, local(): blocks = local_blocks[first_node:first_node + node_count]  5.5 us
    dot_general x1, matrix products, local(): jnp.einsum('lpm,slm->slp', order_hot, panels.reshape(rhs_dev, leaves, lea...  4.75 us
    all_to_all x1, starting transfers between devices, local(): jax.lax.all_to_all(jnp.stack(jnp.split(partial_rows, jax.lax.axis_size('v...  3.63 us
    unnamed x45, local copies, waits for them, and re-layouts  3.58 us
  transfers between devices with their start and end apart: 9, of which 5 were waited for; matrix products, arithmetic and copies ran while one was open for 26% of the time, Pallas kernels for 0%

profile of v1, /device:TPU:0, one launch (start us, length us, event | category | flops | bytes accessed | tf_op | source)
XLA Modules:
  0.0 107.8 jit_solution(13122835773621150606)
XLA Ops:
  6.5 1.4 %slice_bitcast_fusion = f32[32,64,128]{2,1,0:T(8,128)S(1)} fusion(f32[1,63,64,128]{3,2,1,0:T(8,128)} %param.15), kind=kLoop, calls=%fused_computation.35 | loop fusion | bytes 2097152 | tf_op jit(solution)/shard_map/slice | solution.py:93
  9.1 1.2 %slice_bitcast_fusion.6 = f32[8,64,128]{2,1,0:T(8,128)S(1)} fusion(f32[1,63,64,128]{3,2,1,0:T(8,128)} %param.15), kind=kLoop, calls=%fused_computation.53 | loop fusion | bytes 524288 | tf_op jit(solution)/shard_map/slice | solution.py:93
  12.1 4.7 %fusion.2 = f32[64,128,8]{1,2,0:T(8,128)S(1)} fusion(s32[64,128]{1,0:T(8,128)S(1)} %copy-done.18, f32[8,8192]{1,0:T(8,128)S(1)} %copy-done.17), kind=kOutput, calls=%fused_computation.4 | convolution fusion | flops 101711872 | bytes 557056 | tf_op jit(solution)/shard_map/lpm,slm->slp/dot_general | solution.py:65
  16.9 3.4 %bitcast_reduce_fusion = f32[32,8,64]{2,1,0:T(8,128)S(1)} fusion(f32[64,64,128]{2,1,0:T(8,128)S(1)} %copy-done, f32[64,128,8]{1,2,0:T(8,128)S(1)} %fusion.2), kind=kOutput, calls=%fused_computation.49 | convolution fusion | flops 50348032 | bytes 2424832 | tf_op jit(solution)/shard_map/lkp,slp->lsk/dot_general | solution.py:86
  20.2 1.2 %bitcast_reduce_fusion.1 = f32[16,8,64]{2,1,0:T(8,128)S(1)} fusion(f32[32,64,128]{2,1,0:T(8,128)S(1)} %slice_bitcast_fusion, f32[32,8,64]{2,1,0:T(8,128)S(1)} %bitcast_reduce_fusion), kind=kOutput, calls=%fused_computation.58 | convolution fusion | flops 12607488 | bytes 1146880 | tf_op jit(solution)/shard_map/jsk,jkm->jsm/dot_general | solution.py:99
  23.7 3.0 %collective-permute-start.2 = (f32[8,64]{1,0:T(8,128)}, f32[8,64]{1,0:T(8,128)}, u32[]{:S(2)}, u32[]{:S(2)}) collective-permute-start(f32[8,64]{1,0:T(8,128)} %fusion.12), channel_id=1, source_target_pairs={{0,4},{4,0},{8,12},{12,8},{16,20},{20,16},{24,28},{28,24},{1,5},{5... | collective-permute-start | bytes 6152 | tf_op jit(solution)/shard_map/ppermute | solution.py:36
  28.0 1.5 %fusion.68 = f32[8,64]{1,0:T(8,128)} fusion(f32[8,64]{1,0:T(8,128)} %fusion.12, f32[64,128]{1,0:T(8,128)S(1)} %slice_bitcast_fusion.9), kind=kOutput, calls=%fused_computation.89 | convolution fusion | flops 393216 | bytes 36864 | tf_op jit(solution)/shard_map/dot_general | solution.py:103
  32.1 1.9 %convolution_multiply_fusion.3 = f32[4,8,64]{2,1,0:T(8,128)} fusion(f32[4,8,64]{2,1,0:T(8,128)S(1)} %bitcast.154, f32[4,64,128]{2,1,0:T(8,128)} %copy-done.4, f32[4]{0:T(128)S(1)} %slice_bitcast_fusion.11), kind=kOutput, calls=%fused_computation.20 | convolution fusion | flops 1574912 | bytes 147472 | tf_op jit(solution)/shard_map/jkm,jsm->jsk/dot_general | solution.py:97
  34.5 2.0 %convolution_multiply_fusion.1 = f32[16,8,64]{2,1,0:T(8,128)S(1)} fusion(f32[16,8,64]{2,1,0:T(8,128)S(1)} %bitcast.149, f32[16,64,128]{2,1,0:T(8,128)} %copy-done.1, f32[16]{0:T(128)S(1)} %slice_bitcast_fusion.13), kind=kOutput, calls=%fused_computation.16 | convolution fusion | flops 6299648 | bytes 589888 | tf_op jit(solution)/shard_map/jkm,jsm->jsk/dot_general | solution.py:97
  36.5 1.8 %convolution_multiply_fusion = f32[32,8,64]{2,1,0:T(8,128)S(1)} fusion(f32[32,8,64]{2,1,0:T(8,128)S(1)} %bitcast.146, f32[32,64,128]{2,1,0:T(8,128)S(1)} %slice_bitcast_fusion, f32[32]{0:T(128)S(1)} %slice_bitcast_fusion.14), kind=kOutput, calls=%fused_computation.14 | convolution fusion | flops 12599296 | bytes 1179776 | tf_op jit(solution)/shard_map/jkm,jsm->jsk/dot_general | solution.py:97
  39.9 2.1 %collective-permute-start.5 = (f32[8,64]{1,0:T(8,128)S(1)}, f32[8,64]{1,0:T(8,128)S(1)}, u32[]{:S(2)}, u32[]{:S(2)}) collective-permute-start(f32[8,64]{1,0:T(8,128)S(1)} %fusion.55), channel_id=1, source_target_pairs={{0,8},{8,0},{4,12},{12,4},{16,24},{24,16},{20,28},{28,20},{1,9},{9... | collective-permute-start | bytes 6152 | tf_op jit(solution)/shard_map/ppermute | solution.py:36
  42.2 1.4 %collective-permute-done.5 = f32[8,64]{1,0:T(8,128)S(1)} collective-permute-done((f32[8,64]{1,0:T(8,128)S(1)}, f32[8,64]{1,0:T(8,128)S(1)}, u32[]{:S(2)}, u32[]{:S(2)}) %collective-permute-start.5) | collective-permute-done | bytes 2080 | tf_op jit(solution)/shard_map/ppermute | solution.py:36
  43.6 3.0 %collective-permute-start.6 = (f32[8,64]{1,0:T(8,128)S(1)}, f32[8,64]{1,0:T(8,128)S(1)}, u32[]{:S(2)}, u32[]{:S(2)}) collective-permute-start(f32[8,64]{1,0:T(8,128)S(1)} %add_multiply_fusion), channel_id=1, source_target_pairs={{0,16},{16,0},{4,20},{20,4},{8,24},{24,8},{12,28},{28,12},{1,17},{... | collective-permute-start | bytes 6152 | tf_op jit(solution)/shard_map/ppermute | solution.py:36
  46.7 1.3 %slice.157 = f32[1,1]{1,0:T(1,128)} slice(f32[1,63]{1,0:T(1,128)} %copy-done.20), slice={[0:1], [62:63]} | slice | bytes 8 | tf_op jit(solution)/shard_map/slice | solution.py:119
  49.8 1.6 %collective-permute-start.4 = (f32[8,64]{1,0:T(8,128)S(1)}, f32[8,64]{1,0:T(8,128)S(1)}, u32[]{:S(2)}, u32[]{:S(2)}) collective-permute-start(f32[8,64]{1,0:T(8,128)S(1)} %add_multiply_fusion.1), channel_id=1, source_target_pairs={{0,8},{8,0},{4,12},{12,4},{16,24},{24,16},{20,28},{28,20},{1,9},{9... | collective-permute-start | bytes 6152 | tf_op jit(solution)/shard_map/ppermute | solution.py:36
  54.6 1.5 %fusion.11 = f32[8,64]{1,0:T(8,128)S(1)} fusion(f32[8,64]{1,0:T(8,128)S(1)} %fusion.66, f32[8,64]{1,0:T(8,128)} %collective-permute-done.2, f32[64,128]{1,0:T(8,128)S(1)} %copy-done.10, f32[]{:T(128)} %bitcast.39), kind=kOutput, calls=%fused_computation.27 | convolution fusion | flops 394240 | bytes 38916 | tf_op jit(solution)/shard_map/dot_general | solution.py:126
  57.2 1.3 %convolution_add_fusion.3 = f32[4,8,64]{2,1,0:T(8,128)S(1)} fusion(f32[4,8,64]{2,1,0:T(8,128)S(1)} %copy-done.14, f32[4,8,64]{2,1,0:T(8,128)S(1)} %bitcast.155, f32[63,64,128]{2,1,0:T(8,128)} %bitcast.135), kind=kOutput, calls=%fused_computation.19 | convolution fusion | flops 1574912 | bytes 155648 | tf_op jit(solution)/shard_map/jkm,jsm->jsk/dot_general | solution.py:142
  58.5 1.5 %convolution_add_fusion.2 = f32[8,8,64]{2,1,0:T(8,128)S(1)} fusion(f32[8,8,64]{2,1,0:T(8,128)S(1)} %convolution_multiply_fusion.2, f32[8,8,64]{2,1,0:T(8,128)S(1)} %bitcast.153, f32[63,64,128]{2,1,0:T(8,128)} %bitcast.136), kind=kOutput, calls=%fused_computation.17 | convolution fusion | flops 3149824 | bytes 311296 | tf_op jit(solution)/shard_map/jkm,jsm->jsk/dot_general | solution.py:142
  61.2 3.4 %collective-permute-start = (f32[32,1024]{1,0:T(8,128)S(1)}, f32[32,1024]{1,0:T(8,128)S(1)}, u32[]{:S(2)}, u32[]{:S(2)}) collective-permute-start(f32[32,1024]{1,0:T(8,128)S(1)} %get-tuple-element.9), channel_id=1, source_target_pairs={{0,4},{4,8},{8,12},{12,16},{16,20},{20,24},{24,28},{1,5},{5,9},{9,... | collective-permute-start | bytes 393224 | tf_op jit(solution)/shard_map/ppermute | solution.py:20
  64.6 1.5 %collective-permute-start.1 = (f32[32,1024]{1,0:T(8,128)S(1)}, f32[32,1024]{1,0:T(8,128)S(1)}, u32[]{:S(2)}, u32[]{:S(2)}) collective-permute-start(f32[32,1024]{1,0:T(8,128)S(1)} %get-tuple-element.10), channel_id=1, source_target_pairs={{4,0},{8,4},{12,8},{16,12},{20,16},{24,20},{28,24},{5,1},{9,5},{13... | collective-permute-start | bytes 393224 | tf_op jit(solution)/shard_map/ppermute | solution.py:22
  66.1 2.0 %convolution_add_fusion.1 = f32[16,8,64]{2,1,0:T(8,128)S(1)} fusion(f32[16,8,64]{2,1,0:T(8,128)S(1)} %convolution_multiply_fusion.1, f32[16,8,64]{2,1,0:T(8,128)S(1)} %bitcast.150, f32[63,64,128]{2,1,0:T(8,128)} %bitcast.137), kind=kOutput, calls=%fused_computation.15 | convolution fusion | flops 6299648 | bytes 622592 | tf_op jit(solution)/shard_map/jkm,jsm->jsk/dot_general | solution.py:142
  68.5 3.0 %collective-permute-done.1 = f32[32,1024]{1,0:T(8,128)S(1)} collective-permute-done((f32[32,1024]{1,0:T(8,128)S(1)}, f32[32,1024]{1,0:T(8,128)S(1)}, u32[]{:S(2)}, u32[]{:S(2)}) %collective-permute-start.1) | collective-permute-done | bytes 131104 | tf_op jit(solution)/shard_map/ppermute | solution.py:22
  71.8 1.9 %convolution_bitcast_fusion.1 = f32[32,64,4,128]{3,1,2,0:T(8,128)S(1)} fusion(f32[32,80,128,1]{2,1,0,3:T(8,128)S(1)} %bitcast.139, s32[64,4]{0,1:T(4,128)S(1)} %subtract_add_fusion), kind=kOutput, calls=%fused_computation.5 | convolution fusion | flops 1006653440 | bytes 5506048 | tf_op jit(solution)/shard_map/lne,sep->slnp/dot_general | solution.py:76
  74.0 6.2 %fusion.5 = f32[32,64,32]{2,0,1:T(8,128)S(1)} fusion(f32[64,4,32,128]{3,2,1,0:T(8,128)S(1)} %copy-done.2, f32[32,64,4,128]{3,1,2,0:T(8,128)S(1)} %convolution_bitcast_fusion.1), kind=kOutput, calls=%fused_computation.8 | convolution fusion | flops 402653184 | bytes 8650752 | tf_op jit(solution)/shard_map/lnqp,slnp->slq/dot_general | solution.py:40
  80.4 1.2 %copy.16 = f32[4,8,64,32]{2,3,1,0:T(8,128)} copy(f32[4,8,64,32]{3,1,2,0:T(8,128)S(1)} %pad_maximum_fusion) | data formatting | bytes 524288 | tf_op jit(solution)/shard_map/stack | solution.py:80
  81.5 2.1 %reshape.138 = f32[4,1,16384]{2,1,0:T(1,128)} reshape(f32[4,8,32,64]{3,2,1,0:T(8,128)} %bitcast.140) | data formatting | bytes 524288
  83.6 3.6 %all-to-all-start = ((f32[4,1,16384]{2,1,0:T(1,128)}), f32[4,1,16384]{2,1,0:T(1,128)S(1)}, u32[]{:S(2)}, u32[]{:S(2)}) async-start(f32[4,1,16384]{2,1,0:T(1,128)} %reshape.138), calls=%async_computation | async-start | bytes 524288 | tf_op jit(solution)/shard_map/all_to_all | solution.py:79
  87.3 3.0 %convolution_add_fusion = f32[32,8,64]{2,1,0:T(8,128)S(1)} fusion(f32[32,8,64]{2,1,0:T(8,128)S(1)} %convolution_multiply_fusion, f32[32,8,64]{2,1,0:T(8,128)S(1)} %bitcast.147, f32[63,64,128]{2,1,0:T(8,128)} %bitcast.138), kind=kOutput, calls=%fused_computation.13 | convolution fusion | flops 12599296 | bytes 1245184 | tf_op jit(solution)/shard_map/jkm,jsm->jsk/dot_general | solution.py:142
  90.3 2.7 %all-to-all-done = f32[4,1,16384]{2,1,0:T(1,128)S(1)} async-done(((f32[4,1,16384]{2,1,0:T(1,128)}), f32[4,1,16384]{2,1,0:T(1,128)S(1)}, u32[]{:S(2)}, u32[]{:S(2)}) %all-to-all-start) | async-done | bytes 262176 | tf_op jit(solution)/shard_map/all_to_all | solution.py:79
  93.5 1.4 %reduce.2 = f32[4,16384]{1,0:T(4,128)S(1)} reduce(f32[4,1,16384]{2,1,0:T(1,128)S(1)} %all-to-all-done, f32[]{:T(128)} %broadcast.17), dimensions={1}, to_apply=%all_to_all.3.reduce_sub_computation | reduce | bytes 524292 | tf_op jit(solution)/shard_map/all_to_all | solution.py:79
  95.5 1.9 %fusion.9 = f32[8,64,128]{2,0,1:T(8,128)S(1)} fusion(f32[8,64,128]{2,0,1:T(8,128)S(1)} %copy.18, f32[64,8,64]{2,1,0:T(8,128)S(1)} %bitcast.144, f32[64,64,128]{2,1,0:T(8,128)S(1)} %copy-done), kind=kOutput, calls=%fused_computation.12 | convolution fusion | flops 50397184 | bytes 2752512 | tf_op jit(solution)/shard_map/lkp,lsk->slp/dot_general | solution.py:145
  97.4 3.6 %convolution_bitcast_fusion = f32[8,8192]{1,0:T(8,128)} fusion(f32[8,64,128]{2,0,1:T(8,128)S(1)} %fusion.9, s32[64,128]{1,0:T(8,128)S(1)} %copy-done.19), kind=kOutput, calls=%fused_computation | convolution fusion | flops 101711872 | bytes 557056 | tf_op jit(solution)/shard_map/lpm,slp->slm/dot_general | solution.py:149
  (97 shorter events, 19.7 us)
Async XLA Ops:
  6.5 10.3 %copy-start = (f32[64,64,128]{2,1,0:T(8,128)S(1)}, f32[64,64,128]{2,1,0:T(8,128)}, u32[]{:S(2)}) copy-start(f32[64,64,128]{2,1,0:T(8,128)} %param.14) | copy-start | bytes 6291460
  6.5 5.5 %copy-start.18 = (s32[64,128]{1,0:T(8,128)S(1)}, s32[64,128]{1,0:T(8,128)}, u32[]{:S(2)}) copy-start(s32[64,128]{1,0:T(8,128)} %param.13) | copy-start | bytes 98308
  6.5 53.5 %all-gather.2.cloned.1.call-start = ((), (), s32[]{:S(2)}) async-start(), calls=%async_computation.1 | async-start | bytes 1310720 | tf_op jit(solution)/shard_map/all_gather | solution.py:72
  6.5 5.5 %copy-start.17 = (f32[8,8192]{1,0:T(8,128)S(1)}, f32[8,8192]{1,0:T(8,128)}, u32[]{:S(2)}) copy-start(f32[8,8192]{1,0:T(8,128)} %param.10) | copy-start | bytes 786436
  9.1 12.3 %copy-start.1 = (f32[16,64,128]{2,1,0:T(8,128)}, f32[16,64,128]{2,1,0:T(8,128)S(1)}, u32[]{:S(2)}) copy-start(f32[16,64,128]{2,1,0:T(8,128)S(1)} %slice_bitcast_fusion.1) | copy-start | bytes 1572868
  11.2 11.3 %copy-start.4 = (f32[4,64,128]{2,1,0:T(8,128)}, f32[4,64,128]{2,1,0:T(8,128)S(1)}, u32[]{:S(2)}) copy-start(f32[4,64,128]{2,1,0:T(8,128)S(1)} %slice_bitcast_fusion.7) | copy-start | bytes 393220
  12.1 10.7 %copy-start.7 = (f32[2,64,128]{2,1,0:T(8,128)}, f32[2,64,128]{2,1,0:T(8,128)S(1)}, u32[]{:S(2)}) copy-start(f32[2,64,128]{2,1,0:T(8,128)S(1)} %slice_bitcast_fusion.8) | copy-start | bytes 196612
  16.9 5.2 %copy-start.5 = (f32[64,128,8]{1,2,0:T(8,128)}, f32[64,128,8]{1,2,0:T(8,128)S(1)}, u32[]{:S(2)}) copy-start(f32[64,128,8]{1,2,0:T(8,128)S(1)} %fusion.2) | copy-start | bytes 786436
  21.4 1.4 %copy-start.6 = (f32[16,8,64]{2,1,0:T(8,128)}, f32[16,8,64]{2,1,0:T(8,128)S(1)}, u32[]{:S(2)}) copy-start(f32[16,8,64]{2,1,0:T(8,128)S(1)} %bitcast_reduce_fusion.1) | copy-start | bytes 98308
  22.1 1.6 %copy-start.11 = (f32[8,8,64]{2,1,0:T(8,128)}, f32[8,8,64]{2,1,0:T(8,128)S(1)}, u32[]{:S(2)}) copy-start(f32[8,8,64]{2,1,0:T(8,128)S(1)} %bitcast_reduce_fusion.2) | copy-start | bytes 49156
  22.8 6.7 %copy-start.12 = (f32[2,8,64]{2,1,0:T(8,128)}, f32[2,8,64]{2,1,0:T(8,128)S(1)}, u32[]{:S(2)}) copy-start(f32[2,8,64]{2,1,0:T(8,128)S(1)} %bitcast_reduce_fusion.4) | copy-start | bytes 12292
  23.7 30.9 %collective-permute-start.2 = (f32[8,64]{1,0:T(8,128)}, f32[8,64]{1,0:T(8,128)}, u32[]{:S(2)}, u32[]{:S(2)}) collective-permute-start(f32[8,64]{1,0:T(8,128)} %fusion.12), channel_id=1, source_target_pairs={{0,4},{4,0},{8,12},{12,8},{16,20},{20,16},{24,28},{28,24},{1,5},{5... | collective-permute-start | bytes 6152 | tf_op jit(solution)/shard_map/ppermute | solution.py:36
  27.4 0.6 copy-start.9
  29.5 8.8 %collective-permute-start.3 = (f32[8,64]{1,0:T(8,128)}, f32[8,64]{1,0:T(8,128)}, u32[]{:S(2)}, u32[]{:S(2)}) collective-permute-start(f32[8,64]{1,0:T(8,128)} %fusion.68), channel_id=1, source_target_pairs={{0,4},{4,0},{8,12},{12,8},{16,20},{20,16},{24,28},{28,24},{1,5},{5... | collective-permute-start | bytes 6152 | tf_op jit(solution)/shard_map/ppermute | solution.py:36
  30.2 8.1 %copy-start.20 = (f32[1,63]{1,0:T(1,128)}, f32[1,63]{1,0:T(1,128)S(1)}, u32[]{:S(2)}) copy-start(f32[1,63]{1,0:T(1,128)S(1)} %convert_element_type.18) | copy-start | bytes 760
  30.4 7.9 %copy-start.13 = (f32[2,8,64]{2,1,0:T(8,128)S(1)}, f32[2,8,64]{2,1,0:T(8,128)}, u32[]{:S(2)}) copy-start(f32[2,8,64]{2,1,0:T(8,128)} %copy-done.12) | copy-start | bytes 12292
  30.4 16.2 %copy-start.16 = (s32[64,4]{0,1:T(4,128)S(1)}, s32[64,4]{0,1:T(4,128)}, u32[]{:S(2)}) copy-start(s32[64,4]{0,1:T(4,128)} %param.12) | copy-start | bytes 3076
  30.4 17.5 %copy-start.15 = (s32[6]{0:T(128)S(1)}, s32[6]{0:T(128)}, u32[]{:S(2)}) copy-start(s32[6]{0:T(128)} %param.19) | copy-start | bytes 76
  32.1 9.9 %copy-start.8 = (f32[2,64,128]{2,1,0:T(8,128)S(1)}, f32[2,64,128]{2,1,0:T(8,128)}, u32[]{:S(2)}) copy-start(f32[2,64,128]{2,1,0:T(8,128)} %copy-done.7) | copy-start | bytes 196612
  32.1 22.2 %copy-start.10 = (f32[64,128]{1,0:T(8,128)S(1)}, f32[64,128]{1,0:T(8,128)}, u32[]{:S(2)}) copy-start(f32[64,128]{1,0:T(8,128)} %copy-done.9) | copy-start | bytes 98308
  34.5 22.7 %copy-start.14 = (f32[4,8,64]{2,1,0:T(8,128)S(1)}, f32[4,8,64]{2,1,0:T(8,128)}, u32[]{:S(2)}) copy-start(f32[4,8,64]{2,1,0:T(8,128)} %convolution_multiply_fusion.3) | copy-start | bytes 24580
  39.9 3.7 %collective-permute-start.5 = (f32[8,64]{1,0:T(8,128)S(1)}, f32[8,64]{1,0:T(8,128)S(1)}, u32[]{:S(2)}, u32[]{:S(2)}) collective-permute-start(f32[8,64]{1,0:T(8,128)S(1)} %fusion.55), channel_id=1, source_target_pairs={{0,8},{8,0},{4,12},{12,4},{16,24},{24,16},{20,28},{28,20},{1,9},{9... | collective-permute-start | bytes 6152 | tf_op jit(solution)/shard_map/ppermute | solution.py:36
  43.6 7.8 %collective-permute-start.6 = (f32[8,64]{1,0:T(8,128)S(1)}, f32[8,64]{1,0:T(8,128)S(1)}, u32[]{:S(2)}, u32[]{:S(2)}) collective-permute-start(f32[8,64]{1,0:T(8,128)S(1)} %add_multiply_fusion), channel_id=1, source_target_pairs={{0,16},{16,0},{4,20},{20,4},{8,24},{24,8},{12,28},{28,12},{1,17},{... | collective-permute-start | bytes 6152 | tf_op jit(solution)/shard_map/ppermute | solution.py:36
  49.8 3.7 %collective-permute-start.4 = (f32[8,64]{1,0:T(8,128)S(1)}, f32[8,64]{1,0:T(8,128)S(1)}, u32[]{:S(2)}, u32[]{:S(2)}) collective-permute-start(f32[8,64]{1,0:T(8,128)S(1)} %add_multiply_fusion.1), channel_id=1, source_target_pairs={{0,8},{8,0},{4,12},{12,4},{16,24},{24,16},{20,28},{28,20},{1,9},{9... | collective-permute-start | bytes 6152 | tf_op jit(solution)/shard_map/ppermute | solution.py:36
  60.1 11.4 %copy-start.3 = (f32[32,8192]{1,0:T(8,128)S(1)}, f32[32,8192]{1,0:T(8,128)}, u32[]{:S(2)}) copy-start(f32[32,8192]{1,0:T(8,128)} %all-gather.2.cloned.1.call-done) | copy-start | bytes 3145732
  61.2 7.3 %collective-permute-start = (f32[32,1024]{1,0:T(8,128)S(1)}, f32[32,1024]{1,0:T(8,128)S(1)}, u32[]{:S(2)}, u32[]{:S(2)}) collective-permute-start(f32[32,1024]{1,0:T(8,128)S(1)} %get-tuple-element.9), channel_id=1, source_target_pairs={{0,4},{4,8},{8,12},{12,16},{16,20},{20,24},{24,28},{1,5},{5,9},{9,... | collective-permute-start | bytes 393224 | tf_op jit(solution)/shard_map/ppermute | solution.py:20
  64.6 6.9 %collective-permute-start.1 = (f32[32,1024]{1,0:T(8,128)S(1)}, f32[32,1024]{1,0:T(8,128)S(1)}, u32[]{:S(2)}, u32[]{:S(2)}) collective-permute-start(f32[32,1024]{1,0:T(8,128)S(1)} %get-tuple-element.10), channel_id=1, source_target_pairs={{4,0},{8,4},{12,8},{16,12},{20,16},{24,20},{28,24},{5,1},{9,5},{13... | collective-permute-start | bytes 393224 | tf_op jit(solution)/shard_map/ppermute | solution.py:22
  71.8 2.2 %copy-start.2 = (f32[64,4,32,128]{3,2,1,0:T(8,128)S(1)}, f32[64,4,32,128]{3,2,1,0:T(8,128)}, u32[]{:S(2)}) copy-start(f32[64,4,32,128]{3,2,1,0:T(8,128)} %param.11) | copy-start | bytes 12582916
  83.6 9.4 %all-to-all-start = ((f32[4,1,16384]{2,1,0:T(1,128)}), f32[4,1,16384]{2,1,0:T(1,128)S(1)}, u32[]{:S(2)}, u32[]{:S(2)}) async-start(f32[4,1,16384]{2,1,0:T(1,128)} %reshape.138), calls=%async_computation | async-start | bytes 524288 | tf_op jit(solution)/shard_map/all_to_all | solution.py:79
  95.3 2.1 %copy-start.19 = (s32[64,128]{1,0:T(8,128)S(1)}, s32[64,128]{1,0:T(8,128)}, u32[]{:S(2)}) copy-start(s32[64,128]{1,0:T(8,128)} %param.13) | copy-start | bytes 98308
Sparse Core Ops, SparseCore 0:
  29.7 18.5 all-gather.1
